TPU v7x, 32 devices: a whole 2x2x4 slice. The times are simulated.
32 devices in a mesh: dp: 4 (over y, core), seq: 8 (over z, x).
Axes of the slice: x: 2, y: 2, z: 4, core: 2. Of those that a mesh axis runs over, the one named last changes fastest.
Arguments:
- tokens: bfloat16 [8, 1024, 2048], P('dp', 'seq'), may hold values from -6 to 6
- lengths: int32 [8], P('dp'), may hold values from 256 to 1024, as said below
- norm_gain: float32 [2048], replicated, may hold values from 0.5 to 1.5
- in_weight: bfloat16 [2048, 6144], P('seq'), may hold values from -0.125 to 0.125
- conv_taps: float32 [3, 6144], replicated, may hold values from -3 to 3
- filter_residue: float32 [2048, 16], replicated, may hold values from -0.0625 to 0.0625
- filter_decay: float32 [2048, 16], replicated, may hold values from 0.00048828125 to 0.03125
- out_weight: bfloat16 [2048, 2048], P('seq'), may hold values from -0.125 to 0.125
- feed_gain: float32 [2048], replicated, may hold values from 0.5 to 1.5
- gate_weight: bfloat16 [2048, 5632], P('seq'), may hold values from -0.125 to 0.125
- up_weight: bfloat16 [2048, 5632], P('seq'), may hold values from -0.125 to 0.125
- down_weight: bfloat16 [5632, 2048], P('seq'), may hold values from -0.078125 to 0.078125
- cotangent: bfloat16 [8, 1024, 2048], P('dp', 'seq'), may hold values from -6 to 6
Outputs:
- output: bfloat16 [8, 1024, 2048], P('dp', 'seq')
- grad_tokens: bfloat16 [8, 1024, 2048], P('dp', 'seq')
- grad_norm_gain: float32 [2048], replicated
- grad_in_weight: float32 [2048, 6144], P('seq')
- grad_conv_taps: float32 [3, 6144], replicated
- grad_filter_residue: float32 [2048, 16], replicated
- grad_filter_decay: float32 [2048, 16], replicated
- grad_out_weight: float32 [2048, 2048], P('seq')
- grad_feed_gain: float32 [2048], replicated
- grad_gate_weight: float32 [2048, 5632], P('seq')
- grad_up_weight: float32 [2048, 5632], P('seq')
- grad_down_weight: float32 [5632, 2048], P('seq')
Inputs may be any that keep to these rules, and one draw needn't show every extreme that they name: `lengths`: in each aligned block of 2 sequences (those of one index of dp) one sequence is valid to the full 1024 positions.
All inputs are finite; a program needn't handle non-finite values.
Results may differ from a plain program's by a relative error of at most 0.019.
Values may be sent and summed in bfloat16 or wider, within the bound.
No kernel may reach another device: no remote copies, remote signals or barrier semaphores. Data moves between devices by JAX's collectives and lax.ppermute only.
A program may use at most 640 MiB of HBM per device.

v0:
```python
import math
import jax
import jax.numpy as jnp
from jax import lax
from jax.sharding import PartitionSpec as P

epsilon = 1e-06
highest = lax.Precision.HIGHEST


def from_behind(shard, axis, by):
    length = lax.axis_size(axis)
    pairs = [(i, i + by) for i in range(length) if 0 <= i + by < length]
    return lax.ppermute(shard, axis, pairs)


def rms_scale(values):
    return lax.rsqrt(jnp.mean(values * values, axis=-1, keepdims=True) + epsilon)


def norm_back(values, scale, gain, grad_normed):
    grad_gain = jnp.sum(grad_normed * values * scale, axis=(0, 1))
    scaled = grad_normed * gain
    grad_values = scale * scaled - values * scale * scale * scale * jnp.mean(
        scaled * values, axis=-1, keepdims=True
    )
    return (grad_values, grad_gain)


def mode_response(residue, decay, length):
    steps = jnp.arange(length).astype(jnp.float32)
    terms = residue.T[:, None, :] * jnp.exp(-decay.T[:, None, :] * steps[None, :, None])
    return jnp.sum(terms, axis=0)


def split_size(total):
    first = 1
    for option in range(1, math.isqrt(total) + 1):
        if total % option == 0:
            first = option
    return (first, total // first)


def turn_table(rows, cols, modulus):
    index = jnp.arange(rows)[:, None] * jnp.arange(cols)[None, :] % modulus
    angle = index.astype(jnp.float32) * (2.0 * math.pi / modulus)
    return (jnp.cos(angle), jnp.sin(angle))


def complex_mix(spec, table, pair):
    real_table, imag_table = table
    real_part, imag_part = pair
    first = jnp.einsum(spec, real_table, real_part, precision=highest) - jnp.einsum(
        spec, imag_table, imag_part, precision=highest
    )
    second = jnp.einsum(spec, real_table, imag_part, precision=highest) + jnp.einsum(
        spec, imag_table, real_part, precision=highest
    )
    return (first, second)


def complex_times(one, two):
    return (one[0] * two[0] - one[1] * two[1], one[0] * two[1] + one[1] * two[0])


def conjugate(pair):
    return (pair[0], -pair[1])


def spectrum(signal, total):
    batch, length, width = signal.shape
    padded = jnp.pad(signal, ((0, 0), (0, total - length), (0, 0)))
    first, second = split_size(total)
    grid = padded.reshape(batch, second, first, width)
    cosine_inner, sine_inner = turn_table(second, second, second)
    section = (
        jnp.einsum("kn,bnmc->bkmc", cosine_inner, grid, precision=highest),
        -jnp.einsum("kn,bnmc->bkmc", sine_inner, grid, precision=highest),
    )
    cosine_twist, sine_twist = turn_table(second, first, total)
    section = complex_times(
        section, (cosine_twist[None, :, :, None], -sine_twist[None, :, :, None])
    )
    cosine_outer, sine_outer = turn_table(first, first, first)
    result = complex_mix("jm,bkmc->bjkc", (cosine_outer, -sine_outer), section)
    return (result[0].reshape(batch, total, width), result[1].reshape(batch, total, width))


def inverse(pair, total, keep):
    batch = pair[0].shape[0]
    width = pair[0].shape[2]
    first, second = split_size(total)
    grid = (
        pair[0].reshape(batch, first, second, width),
        pair[1].reshape(batch, first, second, width),
    )
    cosine_outer, sine_outer = turn_table(first, first, first)
    section = complex_mix("mj,bjkc->bmkc", (cosine_outer, sine_outer), grid)
    cosine_twist, sine_twist = turn_table(first, second, total)
    section = complex_times(section, (cosine_twist[None, :, :, None], sine_twist[None, :, :, None]))
    cosine_inner, sine_inner = turn_table(second, second, second)
    real = jnp.einsum("nk,bmkc->bnmc", cosine_inner, section[0], precision=highest) - jnp.einsum(
        "nk,bmkc->bnmc", sine_inner, section[1], precision=highest
    )
    return real.reshape(batch, total, width)[:, :keep] / total


def body(
    tokens,
    lengths,
    norm_gain,
    in_weight,
    conv_taps,
    filter_residue,
    filter_decay,
    out_weight,
    feed_gain,
    gate_weight,
    up_weight,
    down_weight,
    cotangent,
):
    parts = lax.axis_size("seq")
    local_len = tokens.shape[1]
    width = tokens.shape[2]
    full_len = local_len * parts
    channels = width // parts
    size = 2 * full_len
    place = lax.axis_index("seq")
    position = place * local_len + jnp.arange(local_len)
    mask = (position[None, :] < lengths[:, None]).astype(jnp.float32)[..., None]
    w_in, w_out, w_gate, w_up, w_down = (
        lax.all_gather(in_weight, "seq", axis=0, tiled=True),
        lax.all_gather(out_weight, "seq", axis=0, tiled=True),
        lax.all_gather(gate_weight, "seq", axis=0, tiled=True),
        lax.all_gather(up_weight, "seq", axis=0, tiled=True),
        lax.all_gather(down_weight, "seq", axis=0, tiled=True),
    )
    hidden = tokens.astype(jnp.float32)
    scale_one = rms_scale(hidden)
    normed = (hidden * scale_one * norm_gain).astype(jnp.bfloat16)
    mixed = jnp.dot(normed, w_in, preferred_element_type=jnp.float32).astype(jnp.bfloat16)
    carried = from_behind(mixed[:, local_len - 2 :, :], "seq", 1)
    extended = jnp.concatenate([carried, mixed], axis=1).astype(jnp.float32)
    short = (
        conv_taps[0] * extended[:, 2:]
        + conv_taps[1] * extended[:, 1:-1]
        + conv_taps[2] * extended[:, :-2]
    )
    query = short[..., :width]
    keys = short[..., width : 2 * width]
    values = short[..., 2 * width :]
    product = (keys * values).astype(jnp.bfloat16)
    product_chan = lax.all_to_all(product, "seq", split_axis=2, concat_axis=1, tiled=True)
    start = place * channels
    residue_part = lax.dynamic_slice_in_dim(filter_residue, start, channels, 0)
    decay_part = lax.dynamic_slice_in_dim(filter_decay, start, channels, 0)
    response = mode_response(residue_part, decay_part, full_len)
    product_spec = spectrum(product_chan.astype(jnp.float32), size)
    response_spec = spectrum(response[None], size)
    conv_chan = inverse(complex_times(product_spec, response_spec), size, full_len)
    convolved = lax.all_to_all(
        conv_chan.astype(jnp.bfloat16), "seq", split_axis=1, concat_axis=2, tiled=True
    ).astype(jnp.float32)
    gated = (query * convolved).astype(jnp.bfloat16)
    middle = hidden + jnp.dot(gated, w_out, preferred_element_type=jnp.float32)
    scale_two = rms_scale(middle)
    normed_two = (middle * scale_two * feed_gain).astype(jnp.bfloat16)
    gate = jnp.dot(normed_two, w_gate, preferred_element_type=jnp.float32)
    upper = jnp.dot(normed_two, w_up, preferred_element_type=jnp.float32)
    sigma = jax.nn.sigmoid(gate)
    active = (gate * sigma * upper).astype(jnp.bfloat16)
    feed = jnp.dot(active, w_down, preferred_element_type=jnp.float32)
    output = (mask * (middle + feed)).astype(jnp.bfloat16)
    grad_out = cotangent.astype(jnp.float32) * mask
    grad_feed = grad_out.astype(jnp.bfloat16)
    grad_active = jnp.einsum("btd,fd->btf", grad_feed, w_down, preferred_element_type=jnp.float32)
    grad_gate = (grad_active * upper * sigma * (1.0 + gate * (1.0 - sigma))).astype(jnp.bfloat16)
    grad_upper = (grad_active * gate * sigma).astype(jnp.bfloat16)
    grad_normed_two = jnp.einsum(
        "btf,df->btd", grad_gate, w_gate, preferred_element_type=jnp.float32
    ) + jnp.einsum("btf,df->btd", grad_upper, w_up, preferred_element_type=jnp.float32)
    term_gate = jnp.einsum("btd,btf->df", normed_two, grad_gate, preferred_element_type=jnp.float32)
    term_up = jnp.einsum("btd,btf->df", normed_two, grad_upper, preferred_element_type=jnp.float32)
    term_down = jnp.einsum("btf,btd->fd", active, grad_feed, preferred_element_type=jnp.float32)
    feed_terms = (
        lax.psum_scatter(
            term_gate.astype(jnp.bfloat16), "seq", scatter_dimension=0, tiled=True
        ).astype(jnp.float32),
        lax.psum_scatter(
            term_up.astype(jnp.bfloat16), "seq", scatter_dimension=0, tiled=True
        ).astype(jnp.float32),
        lax.psum_scatter(
            term_down.astype(jnp.bfloat16), "seq", scatter_dimension=0, tiled=True
        ).astype(jnp.float32),
    )
    grad_middle, grad_feed_gain = norm_back(middle, scale_two, feed_gain, grad_normed_two)
    grad_middle = grad_middle + grad_out
    grad_mix = grad_middle.astype(jnp.bfloat16)
    term_out = jnp.einsum("btd,bte->de", gated, grad_mix, preferred_element_type=jnp.float32)
    grad_gated = jnp.einsum("bte,de->btd", grad_mix, w_out, preferred_element_type=jnp.float32)
    grad_query = grad_gated * convolved
    grad_conv = (grad_gated * query).astype(jnp.bfloat16)
    grad_conv_chan = lax.all_to_all(
        grad_conv, "seq", split_axis=2, concat_axis=1, tiled=True
    ).astype(jnp.float32)
    grad_spec = spectrum(grad_conv_chan, size)
    grad_product_chan = inverse(complex_times(grad_spec, conjugate(response_spec)), size, full_len)
    cross = complex_times(conjugate(product_spec), grad_spec)
    cross = (jnp.sum(cross[0], axis=0, keepdims=True), jnp.sum(cross[1], axis=0, keepdims=True))
    grad_response = inverse(cross, size, full_len)[0]
    grad_product = lax.all_to_all(
        grad_product_chan.astype(jnp.bfloat16), "seq", split_axis=1, concat_axis=2, tiled=True
    ).astype(jnp.float32)
    grad_short = jnp.concatenate([grad_query, grad_product * values, grad_product * keys], axis=-1)
    following = from_behind(grad_short[:, :2, :].astype(jnp.bfloat16), "seq", -1).astype(
        jnp.float32
    )
    grad_extended = jnp.concatenate([grad_short, following], axis=1)
    grad_mixed = (
        conv_taps[0] * grad_extended[:, :local_len]
        + conv_taps[1] * grad_extended[:, 1 : local_len + 1]
        + conv_taps[2] * grad_extended[:, 2:]
    )
    grad_taps = jnp.stack(
        [
            jnp.sum(grad_short * extended[:, 2:], axis=(0, 1)),
            jnp.sum(grad_short * extended[:, 1:-1], axis=(0, 1)),
            jnp.sum(grad_short * extended[:, :-2], axis=(0, 1)),
        ]
    )
    grad_mixed_low = grad_mixed.astype(jnp.bfloat16)
    term_in = jnp.einsum("btd,bte->de", normed, grad_mixed_low, preferred_element_type=jnp.float32)
    grad_normed = jnp.einsum(
        "bte,de->btd", grad_mixed_low, w_in, preferred_element_type=jnp.float32
    )
    mixer_terms = (
        lax.psum_scatter(
            term_in.astype(jnp.bfloat16), "seq", scatter_dimension=0, tiled=True
        ).astype(jnp.float32),
        lax.psum_scatter(
            term_out.astype(jnp.bfloat16), "seq", scatter_dimension=0, tiled=True
        ).astype(jnp.float32),
    )
    grad_hidden, grad_norm_gain = norm_back(hidden, scale_one, norm_gain, grad_normed)
    grad_tokens = (grad_hidden + grad_middle).astype(jnp.bfloat16)

    def response_of(residue_in, decay_in):
        return mode_response(residue_in, decay_in, full_len)

    unused, pull = jax.vjp(response_of, residue_part, decay_part)
    grad_residue_part, grad_decay_part = pull(grad_response)
    grad_residue = lax.dynamic_update_slice_in_dim(
        jnp.zeros_like(filter_residue), grad_residue_part, start, 0
    )
    grad_decay = lax.dynamic_update_slice_in_dim(
        jnp.zeros_like(filter_decay), grad_decay_part, start, 0
    )
    small = lax.psum(
        (grad_norm_gain, grad_taps, grad_residue, grad_decay, grad_feed_gain), ("dp", "seq")
    )
    large = (
        lax.psum(mixer_terms[0].astype(jnp.bfloat16), "dp").astype(jnp.float32),
        lax.psum(mixer_terms[1].astype(jnp.bfloat16), "dp").astype(jnp.float32),
        lax.psum(feed_terms[0].astype(jnp.bfloat16), "dp").astype(jnp.float32),
        lax.psum(feed_terms[1].astype(jnp.bfloat16), "dp").astype(jnp.float32),
        lax.psum(feed_terms[2].astype(jnp.bfloat16), "dp").astype(jnp.float32),
    )
    return (
        output,
        grad_tokens,
        small[0],
        large[0],
        small[1],
        small[2],
        small[3],
        large[1],
        small[4],
        large[2],
        large[3],
        large[4],
    )


def solution(mesh):
    placed = (
        P("dp", "seq", None),
        P("dp"),
        P(),
        P("seq", None),
        P(),
        P(),
        P(),
        P("seq", None),
        P(),
        P("seq", None),
        P("seq", None),
        P("seq", None),
        P("dp", "seq", None),
    )
    return jax.shard_map(
        body,
        mesh=mesh,
        in_specs=placed,
        out_specs=(
            P("dp", "seq", None),
            P("dp", "seq", None),
            P(),
            P("seq", None),
            P(),
            P(),
            P(),
            P("seq", None),
            P(),
            P("seq", None),
            P("seq", None),
            P("seq", None),
        ),
        check_vma=False,
    )
```

profile of v0, /device:TPU:0, one launch (start us, length us, event | category | flops | bytes accessed | tf_op | source)
XLA Modules:
  0.0 4133.8 jit_solution(7491863182339162644)
XLA Ops:
  14.9 4.6 fusion.131
  19.6 473.1 %all-gather.6.cloned.1.call-done = bf16[2048,6144]{1,0:T(8,128)(2,1)} async-done(((bf16[256,6144]{1,0:T(8,128)(2,1)}), bf16[2048,6144]{1,0:T(8,128)(2,1)}) %all-gather.6.cloned.1.call-update) | async-done | bytes 25165840 | tf_op jit(solution)/shard_map/all_gather | solution.py:133
  492.7 11.9 fusion.20
  508.8 25.4 collective-permute-done
  543.8 3.7 copy.168
  547.4 5.6 all-to-all-start
  553.0 6.2 fusion.115
  569.1 15.1 fusion.425
  594.3 4.0 fusion.40
  598.3 7.0 fusion.60
  605.4 6.3 fusion.58
  611.7 6.9 fusion.82
  618.6 6.7 fusion.85
  625.3 4.7 fusion.202
  630.1 4.3 fusion.204
  634.3 5.8 convolution_subtract_fusion.1
  640.2 8.6 fusion.36
  648.7 9.0 fusion.46
  657.7 6.5 subtract_bitcast_fusion.1
  668.9 11.7 all-to-all-start.1
  680.7 277.2 %all-gather.14.cloned.1.call-done = bf16[5632,2048]{1,0:T(8,128)(2,1)} async-done(((bf16[704,2048]{1,0:T(8,128)(2,1)}), bf16[5632,2048]{1,0:T(8,128)(2,1)}) %all-gather.14.cloned.1.call-update) | async-done | bytes 23068688 | tf_op jit(solution)/shard_map/all_gather | solution.py:137
  957.9 13.5 fusion.4
  976.2 109.8 %all-gather.8.cloned.1.call-done = bf16[2048,2048]{1,0:T(8,128)(2,1)} async-done(((bf16[256,2048]{1,0:T(8,128)(2,1)}), bf16[2048,2048]{1,0:T(8,128)(2,1)}) %all-gather.8.cloned.1.call-update) | async-done | bytes 8388624 | tf_op jit(solution)/shard_map/all_gather | solution.py:134
  1085.9 6.2 multiply_reduce_fusion.8
  1092.4 434.2 %all-gather.12.cloned.1.call-done = bf16[2048,5632]{1,0:T(8,128)(2,1)} async-done(((bf16[256,5632]{1,0:T(8,128)(2,1)}), bf16[2048,5632]{1,0:T(8,128)(2,1)}) %all-gather.12.cloned.1.call-update) | async-done | bytes 23068688 | tf_op jit(solution)/shard_map/all_gather | solution.py:136
  1526.7 13.3 fusion.10
  1539.9 429.2 %all-gather.10.cloned.1.call-done = bf16[2048,5632]{1,0:T(8,128)(2,1)} async-done(((bf16[256,5632]{1,0:T(8,128)(2,1)}), bf16[2048,5632]{1,0:T(8,128)(2,1)}) %all-gather.10.cloned.1.call-update) | async-done | bytes 23068688 | tf_op jit(solution)/shard_map/all_gather | solution.py:135
  1969.2 20.0 multiply_convert_fusion.1
  1989.2 12.8 fusion.8
  2001.9 13.7 multiply_reduce_fusion.6
  2019.1 5.7 bitcast_convert_fusion.4
  2024.9 13.1 bitcast_convert_fusion.3
  2038.0 13.2 bitcast_convert_fusion.2
  2052.4 13.2 bitcast_convert_fusion.1
  2065.7 8.6 fusion.423
  2075.0 50.2 %all_to_all.16 = bf16[2,128,2048]{1,0,2:T(2,128)(2,1)S(1)} all-to-all(bf16[2,128,2048]{1,0,2:T(2,128)(2,1)S(1)} %copy.189), channel_id=1, replica_groups=mesh['dp'=4,'seq'=8] {'seq'}, dimensions={2} | all-to-all | bytes 2097152 | tf_op jit(solution)/shard_map/all_to_all | solution.py:204
  2129.1 4.0 fusion.34
  2133.1 7.1 fusion.52
  2140.3 7.0 fusion.50
  2147.3 6.7 fusion.88
  2154.0 15.7 fusion.31
  2169.8 6.5 fusion.196
  2176.3 4.3 fusion.198
  2180.6 6.0 convolution_subtract_fusion
  2186.6 8.7 fusion.26
  2195.3 9.0 fusion.42
  2204.3 6.5 subtract_bitcast_fusion
  2214.5 57.3 %all_to_all.17 = bf16[2,1024,256]{2,0,1:T(2,128)(2,1)S(1)} all-to-all(bf16[2,1024,256]{2,0,1:T(2,128)(2,1)S(1)} %copy.201), channel_id=1, replica_groups=mesh['dp'=4,'seq'=8] {'seq'}, dimensions={1} | all-to-all | bytes 2097152 | tf_op jit(solution)/shard_map/all_to_all | solution.py:212
  2277.1 5.7 collective-permute-done.1
  2286.2 18.1 multiply_reduce_fusion.5
  2304.3 13.9 bitcast_convert_fusion
  2320.0 12.9 fusion.77
  2333.0 262.2 %reduce-scatter.10.cloned.1.call-done = bf16[256,5632]{1,0:T(8,128)(2,1)} async-done(((bf16[2048,5632]{1,0:T(8,128)(2,1)}), bf16[256,5632]{1,0:T(8,128)(2,1)}) %reduce-scatter.10.cloned.1.call-update) | async-done | bytes 2883600 | tf_op jit(solution)/shard_map/reduce_scatter | solution.py:187
  2595.1 377.1 %reduce-scatter.12.cloned.1.call-done = bf16[256,5632]{1,0:T(8,128)(2,1)} async-done(((bf16[2048,5632]{1,0:T(8,128)(2,1)}), bf16[256,5632]{1,0:T(8,128)(2,1)}) %reduce-scatter.12.cloned.1.call-update) | async-done | bytes 2883600 | tf_op jit(solution)/shard_map/reduce_scatter | solution.py:190
  2972.2 377.0 %reduce-scatter.14.cloned.1.call-done = bf16[704,2048]{1,0:T(8,128)(2,1)} async-done(((bf16[5632,2048]{1,0:T(8,128)(2,1)}), bf16[704,2048]{1,0:T(8,128)(2,1)}) %reduce-scatter.14.cloned.1.call-update) | async-done | bytes 2883600 | tf_op jit(solution)/shard_map/reduce_scatter | solution.py:193
  3349.2 407.1 %reduce-scatter.6.cloned.1.call-done = bf16[256,6144]{1,0:T(8,128)(2,1)} async-done(((bf16[2048,6144]{1,0:T(8,128)(2,1)}), bf16[256,6144]{1,0:T(8,128)(2,1)}) %reduce-scatter.6.cloned.1.call-update) | async-done | bytes 3145744 | tf_op jit(solution)/shard_map/reduce_scatter | solution.py:238
  3766.8 3.6 fusion.118
  3770.4 3.5 subtract_bitcast_fusion.2
  3775.3 5.7 multiply_reduce_fusion
  3781.1 13.9 fusion.107
  3799.1 41.1 all-reduce.3
  3840.2 146.3 %all-reduce.11.cloned.1.call-done = (bf16[256,6144]{1,0:T(8,128)(2,1)}, bf16[256,2048]{1,0:T(8,128)(2,1)}, bf16[256,5632]{1,0:T(8,128)(2,1)}, bf16[256,5632]{1,0:T(8,128)(2,1)}, bf16[704,2048]{1,0:T(8,128)(2,1)}) async-done(((bf16[256,6144]{1,0:T(8,128)(2,1)}, bf16[256,2048]{1,0:T(8,128)(2,1)}, bf16[256,5632]{1,0:T(8,128)(2,1)}, bf16[256,5632]{1,0:T(8,128)(2,1)}, bf16[704,2048]{1,0:T(8,128)(2,1)}), ...) | async-done | bytes 12845072 | tf_op jit(solution)/shard_map/psum | solution.py:263
  3986.5 5.5 convert_element_type.355
  4003.3 118.5 %all-reduce.9.cloned.1.call-done = (f32[3,6144]{1,0:T(4,128)}, f32[2048,16]{0,1:T(8,128)}, f32[2048,16]{0,1:T(8,128)}) async-done(((f32[3,6144]{1,0:T(4,128)}, f32[2048,16]{0,1:T(8,128)}, f32[2048,16]{0,1:T(8,128)}), (f32[3,6144]{1,0:T(4,128)}, f32[2048,16]{0,1:T(8,128)}, f32[2048,16]{0,1:T(8,128)})) %all-reduce.9.cloned.1.call-update) | async-done | bytes 335888 | tf_op jit(solution)/shard_map/psum | solution.py:259
  (225 shorter events, 106.2 us)
Async XLA Ops:
  7.2 485.5 %all-gather.6.cloned.1.call-start = ((), (), s32[]{:S(2)}) async-start(), calls=%async_computation.9 | async-start | bytes 28311552 | tf_op jit(solution)/shard_map/all_gather | solution.py:133
  7.9 950.0 %all-gather.14.cloned.1.call-start = ((), (), s32[]{:S(2)}) async-start(), calls=%async_computation.13 | async-start | bytes 25952256 | tf_op jit(solution)/shard_map/all_gather | solution.py:137
  8.7 1077.3 %all-gather.8.cloned.1.call-start = ((), (), s32[]{:S(2)}) async-start(), calls=%async_computation.10 | async-start | bytes 9437184 | tf_op jit(solution)/shard_map/all_gather | solution.py:134
  9.4 1517.3 %all-gather.12.cloned.1.call-start = ((), (), s32[]{:S(2)}) async-start(), calls=%async_computation.12 | async-start | bytes 25952256 | tf_op jit(solution)/shard_map/all_gather | solution.py:136
  10.0 1959.2 %all-gather.10.cloned.1.call-start = ((), (), s32[]{:S(2)}) async-start(), calls=%async_computation.11 | async-start | bytes 25952256 | tf_op jit(solution)/shard_map/all_gather | solution.py:135
  10.6 3.8 copy-start.58
  11.4 3.1 copy-start.55
  11.4 3.2 copy-start.19
  14.2 5.3 copy-start.49
  14.2 478.5 %copy-start.47 = (f32[2048]{0:T(1024)S(1)}, f32[2048]{0:T(1024)}, u32[]{:S(2)}) copy-start(f32[2048]{0:T(1024)} %param.15) | copy-start | bytes 24580
  14.6 625.5 %copy-start.30 = (f32[32,64]{0,1:T(8,128)}, f32[32,64]{0,1:T(8,128)S(1)}, u32[]{:S(2)}) copy-start(f32[32,64]{0,1:T(8,128)S(1)} %get-tuple-element.67) | copy-start | bytes 24580
  14.6 625.5 %copy-start.32 = (f32[32,64]{0,1:T(8,128)}, f32[32,64]{0,1:T(8,128)S(1)}, u32[]{:S(2)}) copy-start(f32[32,64]{0,1:T(8,128)S(1)} %get-tuple-element.68) | copy-start | bytes 24580
  14.9 489.7 %copy-start.50 = (f32[2,128]{1,0:T(2,128)}, f32[2,128]{1,0:T(2,128)S(1)}, u32[]{:S(2)}) copy-start(f32[2,128]{1,0:T(2,128)S(1)} %add_rsqrt_fusion.1) | copy-start | bytes 3076
  19.6 517.5 %copy-start.41 = (f32[1,6144]{1,0:T(1,128)}, f32[1,6144]{1,0:T(1,128)S(1)}, u32[]{:S(2)}) copy-start(f32[1,6144]{1,0:T(1,128)S(1)} %get-tuple-element.53) | copy-start | bytes 73732
  19.6 517.5 %copy-start.43 = (f32[1,6144]{1,0:T(1,128)}, f32[1,6144]{1,0:T(1,128)S(1)}, u32[]{:S(2)}) copy-start(f32[1,6144]{1,0:T(1,128)S(1)} %get-tuple-element.54) | copy-start | bytes 73732
  19.6 517.5 %copy-start.45 = (f32[1,6144]{1,0:T(1,128)}, f32[1,6144]{1,0:T(1,128)S(1)}, u32[]{:S(2)}) copy-start(f32[1,6144]{1,0:T(1,128)S(1)} %get-tuple-element.55) | copy-start | bytes 73732
  506.3 27.9 collective-permute-start
  508.8 85.5 %copy-start.37 = (f32[64,32]{0,1:T(8,128)}, f32[64,32]{0,1:T(8,128)S(1)}, u32[]{:S(2)}) copy-start(f32[64,32]{0,1:T(8,128)S(1)} %get-tuple-element.63) | copy-start | bytes 24580
  508.8 85.5 %copy-start.39 = (f32[64,32]{0,1:T(8,128)}, f32[64,32]{0,1:T(8,128)S(1)}, u32[]{:S(2)}) copy-start(f32[64,32]{0,1:T(8,128)S(1)} %get-tuple-element.64) | copy-start | bytes 24580
  547.4 38.1 all-to-all-start
  569.1 71.0 %copy-start = (f32[32,64,256]{2,0,1:T(8,128)}, f32[32,64,256]{2,0,1:T(8,128)S(1)}, u32[]{:S(2)}) copy-start(f32[32,64,256]{2,0,1:T(8,128)S(1)} %subtract_bitcast_fusion.3) | copy-start | bytes 6291460
  618.6 21.5 copy-start.3
  618.6 6.7 copy-start.8
  625.3 14.8 copy-start.5
  666.6 14.0 copy-start.60
  666.6 291.3 %copy-start.24 = (bf16[2,128,2048]{2,1,0:T(8,128)(2,1)S(1)}, bf16[2,128,2048]{2,1,0:T(8,128)(2,1)}, u32[]{:S(2)}) copy-start(bf16[2,128,2048]{2,1,0:T(8,128)(2,1)} %param.25) | copy-start | bytes 3145732
  668.9 302.5 %all-to-all-start.1 = ((bf16[2,1024,256]{2,0,1:T(2,128)(2,1)}), bf16[2,1024,256]{2,0,1:T(2,128)(2,1)S(1)}, u32[]{:S(2)}, u32[]{:S(2)}) async-start(bf16[2,1024,256]{2,0,1:T(2,128)(2,1)} %copy.186), calls=%async_computation.1 | async-start | bytes 2097152 | tf_op jit(solution)/shard_map/all_to_all | solution.py:162
  680.6 1652.4 %reduce-scatter.8.cloned.1.call-start = ((), (), s32[]{:S(2)}) async-start(), calls=%async_computation.15 | async-start | bytes 9437184 | tf_op jit(solution)/shard_map/reduce_scatter | solution.py:241
  976.2 116.0 %copy-start.52 = (f32[2048]{0:T(1024)S(1)}, f32[2048]{0:T(1024)}, u32[]{:S(2)}) copy-start(f32[2048]{0:T(1024)} %param.21) | copy-start | bytes 24580
  1092.1 909.8 %copy-start.21 = (f32[2,128,2048]{2,1,0:T(8,128)}, f32[2,128,2048]{2,1,0:T(8,128)S(1)}, u32[]{:S(2)}) copy-start(f32[2,128,2048]{2,1,0:T(8,128)S(1)} %get-tuple-element.57) | copy-start | bytes 6291460
  2015.7 3.4 copy-start.23
  2019.1 46.6 %copy-start.11 = (f32[2,128,2048]{2,1,0:T(8,128)}, f32[2,128,2048]{2,1,0:T(8,128)S(1)}, u32[]{:S(2)}) copy-start(f32[2,128,2048]{2,1,0:T(8,128)S(1)} %subtract_add_fusion) | copy-start | bytes 6291460
  2024.8 570.3 %reduce-scatter.10.cloned.1.call-start = ((), (), s32[]{:S(2)}) async-start(), calls=%async_computation.16 | async-start | bytes 25952256 | tf_op jit(solution)/shard_map/reduce_scatter | solution.py:187
  2037.9 934.3 %reduce-scatter.12.cloned.1.call-start = ((), (), s32[]{:S(2)}) async-start(), calls=%async_computation.17 | async-start | bytes 25952256 | tf_op jit(solution)/shard_map/reduce_scatter | solution.py:190
  2051.2 1298.0 %reduce-scatter.14.cloned.1.call-start = ((), (), s32[]{:S(2)}) async-start(), calls=%async_computation.18 | async-start | bytes 25952256 | tf_op jit(solution)/shard_map/reduce_scatter | solution.py:193
  2065.6 1690.6 %reduce-scatter.6.cloned.1.call-start = ((), (), s32[]{:S(2)}) async-start(), calls=%async_computation.14 | async-start | bytes 28311552 | tf_op jit(solution)/shard_map/reduce_scatter | solution.py:238
  2133.1 14.2 copy-start.9
  2147.3 6.7 copy-start.4
  2147.3 6.7 copy-start.6
  2154.0 15.8 copy-start.1
  2169.8 6.5 copy-start.7
  2180.6 6.0 copy-start.31
  2180.6 6.0 copy-start.33
  2213.2 59.2 %slice-start = ((s8[6291456]{0:T(1024)(128)(4,1)}), s8[4194304]{0:T(1024)(128)(4,1)S(1)}, s32[]{:S(2)}) async-start(s8[6291456]{0:T(1024)(128)(4,1)} %bitcast.429), calls=%async_computation.21 | async-start | bytes 8388608
  2274.5 8.3 copy-start.14
  2274.5 8.3 copy-start.15
  2275.8 7.0 collective-permute-start.1
  2282.8 3.4 copy-start.42
  2282.9 3.4 copy-start.44
  2282.9 3.3 copy-start.46
  2286.2 18.1 copy-start.20
  2286.2 18.1 copy-start.48
  2286.2 18.1 copy-start.51
  2318.2 1668.3 %all-reduce.11.cloned.1.call-start = ((), (), s32[]{:S(2)}) async-start(), calls=%async_computation.20 | async-start | bytes 25690112 | tf_op jit(solution)/shard_map/psum | solution.py:263
  3756.3 365.4 %all-reduce.9.cloned.1.call-start = ((), (), s32[]{:S(2)}) async-start(), calls=%async_computation.19 | async-start | bytes 720896 | tf_op jit(solution)/shard_map/psum | solution.py:259
  3756.5 3.3 copy-start.17
  3781.0 14.0 copy-start.36
  3781.1 14.0 copy-start.35
  3781.1 14.7 copy-start.12
  3795.1 4.1 copy-start.57
  3986.5 5.5 copy-start.29
  3992.0 3.2 copy-start.28
  3995.2 3.2 copy-start.27
  3998.4 3.3 copy-start.34
  (15 other events, 29.5 us)
Sparse Core Ops, SparseCore 0:
  9.5 483.1 all-gather.5
  494.2 463.6 all-gather.13
  960.0 125.8 all-gather.7
  1087.3 439.2 all-gather.11
  1528.0 441.0 all-gather.9
  2024.9 169.6 reduce-scatter.7
  2199.0 396.0 reduce-scatter.9
  2599.5 372.6 reduce-scatter.11
  2976.6 372.5 reduce-scatter.13
  3353.4 402.8 reduce-scatter.5
  3759.6 226.8 all-reduce.10
  3993.6 128.0 all-reduce.8
where the time goes:
time: 4140 us; the launch traced here: 4130 us
  waiting for transfers between devices  3450 us (83%)
  matrix products  394 us (10%)
  blocking collectives  149 us (4%)
  other arithmetic  66.7 us (2%)
    all_gather x1, waiting for transfers between devices, body(): lax.all_gather(in_weight, 'seq', axis=0, tiled=True)  473 us
    all_gather x1, waiting for transfers between devices, body(): lax.all_gather(up_weight, 'seq', axis=0, tiled=True)  434 us
    all_gather x1, waiting for transfers between devices, body(): lax.all_gather(gate_weight, 'seq', axis=0, tiled=True)  429 us
    reduce_scatter x1, waiting for transfers between devices, body(): lax.psum_scatter(term_in.astype(jnp.bfloat16), 'seq', scatter_dimension=0...  407 us
    reduce_scatter x1, waiting for transfers between devices, body(): lax.psum_scatter(term_up.astype(jnp.bfloat16), 'seq', scatter_dimension=0...  377 us
    reduce_scatter x1, waiting for transfers between devices, body(): lax.psum_scatter(term_down.astype(jnp.bfloat16), 'seq', scatter_dimension...  377 us
    all_gather x1, waiting for transfers between devices, body(): lax.all_gather(down_weight, 'seq', axis=0, tiled=True)  277 us
    reduce_scatter x1, waiting for transfers between devices, body(): lax.psum_scatter(term_gate.astype(jnp.bfloat16), 'seq', scatter_dimension...  262 us
  transfers between devices with their start and end apart: 16, of which 14 were waited for; matrix products, arithmetic and copies ran while one was open for 10% of the time, Pallas kernels for 0%

commit v1 on v0

--- a/solution.py
+++ b/solution.py
@@ -256,9 +256,9 @@
     grad_decay = lax.dynamic_update_slice_in_dim(
         jnp.zeros_like(filter_decay), grad_decay_part, start, 0
     )
-    small = lax.psum(
-        (grad_norm_gain, grad_taps, grad_residue, grad_decay, grad_feed_gain), ("dp", "seq")
-    )
+    small = (grad_norm_gain, grad_taps, grad_residue, grad_decay, grad_feed_gain)
+    for mesh_axis in ("seq", "dp"):
+        small = lax.psum(small, mesh_axis)
     large = (
         lax.psum(mixer_terms[0].astype(jnp.bfloat16), "dp").astype(jnp.float32),
         lax.psum(mixer_terms[1].astype(jnp.bfloat16), "dp").astype(jnp.float32),

time: 4140 us -> 4120 us (level)
    psum x1 -> x2, waiting for transfers between devices: 118 us -> 66.3 us  [body(): small = lax.psum(small, mesh_axis)]
  transfers between devices with their start and end apart: 16 -> 17, of which waited for: 14 -> 15; matrix products, arithmetic and copies ran while one was open for 10% -> 10% of each run, Pallas kernels for 0% -> 0%
where the time goes in v1:
time: 4120 us; the launch traced here: 4110 us
  waiting for transfers between devices  3420 us (83%)
  matrix products  394 us (10%)
  blocking collectives  156 us (4%)
  other arithmetic  66.7 us (2%)
    all_gather x1, waiting for transfers between devices, body(): lax.all_gather(in_weight, 'seq', axis=0, tiled=True)  473 us
    all_gather x1, waiting for transfers between devices, body(): lax.all_gather(up_weight, 'seq', axis=0, tiled=True)  434 us
    all_gather x1, waiting for transfers between devices, body(): lax.all_gather(gate_weight, 'seq', axis=0, tiled=True)  429 us
    reduce_scatter x1, waiting for transfers between devices, body(): lax.psum_scatter(term_in.astype(jnp.bfloat16), 'seq', scatter_dimension=0...  407 us
    reduce_scatter x1, waiting for transfers between devices, body(): lax.psum_scatter(term_down.astype(jnp.bfloat16), 'seq', scatter_dimension...  377 us
    reduce_scatter x1, waiting for transfers between devices, body(): lax.psum_scatter(term_up.astype(jnp.bfloat16), 'seq', scatter_dimension=0...  377 us
    all_gather x1, waiting for transfers between devices, body(): lax.all_gather(down_weight, 'seq', axis=0, tiled=True)  277 us
    reduce_scatter x1, waiting for transfers between devices, body(): lax.psum_scatter(term_gate.astype(jnp.bfloat16), 'seq', scatter_dimension...  251 us
  transfers between devices with their start and end apart: 17, of which 15 were waited for; matrix products, arithmetic and copies ran while one was open for 10% of the time, Pallas kernels for 0%

profile of v1, /device:TPU:0, one launch (start us, length us, event | category | flops | bytes accessed | tf_op | source)
XLA Modules:
  0.0 4107.6 jit_solution(5634616393108580330)
XLA Ops:
  14.9 4.6 fusion.131
  19.6 473.1 %all-gather.6.cloned.1.call-done = bf16[2048,6144]{1,0:T(8,128)(2,1)} async-done(((bf16[256,6144]{1,0:T(8,128)(2,1)}), bf16[2048,6144]{1,0:T(8,128)(2,1)}) %all-gather.6.cloned.1.call-update) | async-done | bytes 25165840 | tf_op jit(solution)/shard_map/all_gather | solution.py:133
  492.7 11.9 fusion.20
  508.8 25.4 collective-permute-done
  543.8 3.7 copy.168
  547.5 5.6 all-to-all-start
  553.1 6.2 fusion.115
  569.2 15.1 fusion.425
  594.5 4.0 fusion.40
  598.5 7.0 fusion.60
  605.6 6.3 fusion.58
  611.9 6.9 fusion.82
  618.8 6.7 fusion.85
  625.5 4.7 fusion.202
  630.3 4.3 fusion.204
  634.6 5.8 convolution_subtract_fusion.1
  640.4 8.6 fusion.36
  648.9 9.0 fusion.46
  657.9 6.5 subtract_bitcast_fusion.1
  669.1 11.6 all-to-all-start.1
  680.8 277.1 %all-gather.14.cloned.1.call-done = bf16[5632,2048]{1,0:T(8,128)(2,1)} async-done(((bf16[704,2048]{1,0:T(8,128)(2,1)}), bf16[5632,2048]{1,0:T(8,128)(2,1)}) %all-gather.14.cloned.1.call-update) | async-done | bytes 23068688 | tf_op jit(solution)/shard_map/all_gather | solution.py:137
  957.9 13.5 fusion.4
  976.2 109.8 %all-gather.8.cloned.1.call-done = bf16[2048,2048]{1,0:T(8,128)(2,1)} async-done(((bf16[256,2048]{1,0:T(8,128)(2,1)}), bf16[2048,2048]{1,0:T(8,128)(2,1)}) %all-gather.8.cloned.1.call-update) | async-done | bytes 8388624 | tf_op jit(solution)/shard_map/all_gather | solution.py:134
  1085.9 6.2 multiply_reduce_fusion.8
  1092.4 434.2 %all-gather.12.cloned.1.call-done = bf16[2048,5632]{1,0:T(8,128)(2,1)} async-done(((bf16[256,5632]{1,0:T(8,128)(2,1)}), bf16[2048,5632]{1,0:T(8,128)(2,1)}) %all-gather.12.cloned.1.call-update) | async-done | bytes 23068688 | tf_op jit(solution)/shard_map/all_gather | solution.py:136
  1526.7 13.3 fusion.10
  1539.9 429.2 %all-gather.10.cloned.1.call-done = bf16[2048,5632]{1,0:T(8,128)(2,1)} async-done(((bf16[256,5632]{1,0:T(8,128)(2,1)}), bf16[2048,5632]{1,0:T(8,128)(2,1)}) %all-gather.10.cloned.1.call-update) | async-done | bytes 23068688 | tf_op jit(solution)/shard_map/all_gather | solution.py:135
  1969.2 20.1 multiply_convert_fusion.1
  1989.2 12.8 fusion.8
  2002.0 13.8 multiply_reduce_fusion.6
  2019.3 5.7 bitcast_convert_fusion.4
  2025.0 13.1 bitcast_convert_fusion.3
  2038.2 13.2 bitcast_convert_fusion.2
  2052.6 13.1 bitcast_convert_fusion.1
  2065.8 8.6 fusion.423
  2075.2 50.3 %all_to_all.16 = bf16[2,128,2048]{1,0,2:T(2,128)(2,1)S(1)} all-to-all(bf16[2,128,2048]{1,0,2:T(2,128)(2,1)S(1)} %copy.189), channel_id=1, replica_groups=mesh['dp'=4,'seq'=8] {'seq'}, dimensions={2} | all-to-all | bytes 2097152 | tf_op jit(solution)/shard_map/all_to_all | solution.py:204
  2129.3 4.0 fusion.34
  2133.3 7.1 fusion.52
  2140.5 7.0 fusion.50
  2147.5 6.7 fusion.88
  2154.2 15.7 fusion.31
  2169.9 6.5 fusion.196
  2176.4 4.3 fusion.198
  2180.7 6.0 convolution_subtract_fusion
  2186.7 8.7 fusion.26
  2195.5 9.0 fusion.42
  2204.5 6.5 subtract_bitcast_fusion
  2214.7 57.4 %all_to_all.17 = bf16[2,1024,256]{2,0,1:T(2,128)(2,1)S(1)} all-to-all(bf16[2,1024,256]{2,0,1:T(2,128)(2,1)S(1)} %copy.201), channel_id=1, replica_groups=mesh['dp'=4,'seq'=8] {'seq'}, dimensions={1} | all-to-all | bytes 2097152 | tf_op jit(solution)/shard_map/all_to_all | solution.py:212
  2277.3 5.9 collective-permute-done.1
  2286.7 18.0 multiply_reduce_fusion.5
  2304.7 13.8 bitcast_convert_fusion
  2337.7 5.7 multiply_reduce_fusion
  2344.3 251.0 %reduce-scatter.10.cloned.1.call-done = bf16[256,5632]{1,0:T(8,128)(2,1)} async-done(((bf16[2048,5632]{1,0:T(8,128)(2,1)}), bf16[256,5632]{1,0:T(8,128)(2,1)}) %reduce-scatter.10.cloned.1.call-update) | async-done | bytes 2883600 | tf_op jit(solution)/shard_map/reduce_scatter | solution.py:187
  2595.4 376.5 %reduce-scatter.12.cloned.1.call-done = bf16[256,5632]{1,0:T(8,128)(2,1)} async-done(((bf16[2048,5632]{1,0:T(8,128)(2,1)}), bf16[256,5632]{1,0:T(8,128)(2,1)}) %reduce-scatter.12.cloned.1.call-update) | async-done | bytes 2883600 | tf_op jit(solution)/shard_map/reduce_scatter | solution.py:190
  2971.9 377.1 %reduce-scatter.14.cloned.1.call-done = bf16[704,2048]{1,0:T(8,128)(2,1)} async-done(((bf16[5632,2048]{1,0:T(8,128)(2,1)}), bf16[704,2048]{1,0:T(8,128)(2,1)}) %reduce-scatter.14.cloned.1.call-update) | async-done | bytes 2883600 | tf_op jit(solution)/shard_map/reduce_scatter | solution.py:193
  3349.0 407.2 %reduce-scatter.6.cloned.1.call-done = bf16[256,6144]{1,0:T(8,128)(2,1)} async-done(((bf16[2048,6144]{1,0:T(8,128)(2,1)}), bf16[256,6144]{1,0:T(8,128)(2,1)}) %reduce-scatter.6.cloned.1.call-update) | async-done | bytes 3145744 | tf_op jit(solution)/shard_map/reduce_scatter | solution.py:238
  3757.7 12.4 fusion.77
  3770.1 14.0 fusion.107
  3784.1 47.6 %all-reduce.12.cloned.1.call-done = (f32[3,6144]{1,0:T(4,128)}, f32[2048,16]{0,1:T(8,128)}, f32[2048,16]{0,1:T(8,128)}) async-done(((f32[3,6144]{1,0:T(4,128)}, f32[2048,16]{0,1:T(8,128)}, f32[2048,16]{0,1:T(8,128)}), (f32[3,6144]{1,0:T(4,128)}, f32[2048,16]{0,1:T(8,128)}, f32[2048,16]{0,1:T(8,128)})) %all-reduce.12.cloned.1.call-update) | async-done | bytes 335888 | tf_op jit(solution)/shard_map/psum | solution.py:261
  3835.1 35.4 all-reduce.3
  3870.5 12.5 all-reduce.5
  3883.0 177.5 %all-reduce.16.cloned.1.call-done = (bf16[256,6144]{1,0:T(8,128)(2,1)}, bf16[256,2048]{1,0:T(8,128)(2,1)}, bf16[256,5632]{1,0:T(8,128)(2,1)}, bf16[256,5632]{1,0:T(8,128)(2,1)}, bf16[704,2048]{1,0:T(8,128)(2,1)}) async-done(((bf16[256,6144]{1,0:T(8,128)(2,1)}, bf16[256,2048]{1,0:T(8,128)(2,1)}, bf16[256,5632]{1,0:T(8,128)(2,1)}, bf16[256,5632]{1,0:T(8,128)(2,1)}, bf16[704,2048]{1,0:T(8,128)(2,1)}), ...) | async-done | bytes 12845072 | tf_op jit(solution)/shard_map/psum | solution.py:263
  4060.6 5.5 convert_element_type.355
  4077.3 18.6 all-reduce.14.cloned.1.call-done
  (229 shorter events, 113.7 us)
Async XLA Ops:
  7.2 485.5 %all-gather.6.cloned.1.call-start = ((), (), s32[]{:S(2)}) async-start(), calls=%async_computation.9 | async-start | bytes 28311552 | tf_op jit(solution)/shard_map/all_gather | solution.py:133
  7.9 950.0 %all-gather.14.cloned.1.call-start = ((), (), s32[]{:S(2)}) async-start(), calls=%async_computation.13 | async-start | bytes 25952256 | tf_op jit(solution)/shard_map/all_gather | solution.py:137
  8.7 1077.3 %all-gather.8.cloned.1.call-start = ((), (), s32[]{:S(2)}) async-start(), calls=%async_computation.10 | async-start | bytes 9437184 | tf_op jit(solution)/shard_map/all_gather | solution.py:134
  9.4 1517.3 %all-gather.12.cloned.1.call-start = ((), (), s32[]{:S(2)}) async-start(), calls=%async_computation.12 | async-start | bytes 25952256 | tf_op jit(solution)/shard_map/all_gather | solution.py:136
  10.0 1959.2 %all-gather.10.cloned.1.call-start = ((), (), s32[]{:S(2)}) async-start(), calls=%async_computation.11 | async-start | bytes 25952256 | tf_op jit(solution)/shard_map/all_gather | solution.py:135
  10.6 3.8 copy-start.58
  11.4 3.0 copy-start.53
  11.4 3.1 copy-start.55
  11.4 3.2 copy-start.19
  14.2 5.3 copy-start.49
  14.2 478.5 %copy-start.47 = (f32[2048]{0:T(1024)S(1)}, f32[2048]{0:T(1024)}, u32[]{:S(2)}) copy-start(f32[2048]{0:T(1024)} %param.15) | copy-start | bytes 24580
  14.6 625.8 %copy-start.30 = (f32[32,64]{0,1:T(8,128)}, f32[32,64]{0,1:T(8,128)S(1)}, u32[]{:S(2)}) copy-start(f32[32,64]{0,1:T(8,128)S(1)} %get-tuple-element.72) | copy-start | bytes 24580
  14.6 625.7 %copy-start.32 = (f32[32,64]{0,1:T(8,128)}, f32[32,64]{0,1:T(8,128)S(1)}, u32[]{:S(2)}) copy-start(f32[32,64]{0,1:T(8,128)S(1)} %get-tuple-element.73) | copy-start | bytes 24580
  14.9 489.7 %copy-start.50 = (f32[2,128]{1,0:T(2,128)}, f32[2,128]{1,0:T(2,128)S(1)}, u32[]{:S(2)}) copy-start(f32[2,128]{1,0:T(2,128)S(1)} %add_rsqrt_fusion.1) | copy-start | bytes 3076
  19.6 517.5 %copy-start.41 = (f32[1,6144]{1,0:T(1,128)}, f32[1,6144]{1,0:T(1,128)S(1)}, u32[]{:S(2)}) copy-start(f32[1,6144]{1,0:T(1,128)S(1)} %get-tuple-element.58) | copy-start | bytes 73732
  19.6 517.5 %copy-start.43 = (f32[1,6144]{1,0:T(1,128)}, f32[1,6144]{1,0:T(1,128)S(1)}, u32[]{:S(2)}) copy-start(f32[1,6144]{1,0:T(1,128)S(1)} %get-tuple-element.59) | copy-start | bytes 73732
  19.6 517.5 %copy-start.45 = (f32[1,6144]{1,0:T(1,128)}, f32[1,6144]{1,0:T(1,128)S(1)}, u32[]{:S(2)}) copy-start(f32[1,6144]{1,0:T(1,128)S(1)} %get-tuple-element.60) | copy-start | bytes 73732
  506.3 27.9 collective-permute-start
  508.8 85.7 %copy-start.37 = (f32[64,32]{0,1:T(8,128)}, f32[64,32]{0,1:T(8,128)S(1)}, u32[]{:S(2)}) copy-start(f32[64,32]{0,1:T(8,128)S(1)} %get-tuple-element.68) | copy-start | bytes 24580
  508.8 85.7 %copy-start.39 = (f32[64,32]{0,1:T(8,128)}, f32[64,32]{0,1:T(8,128)S(1)}, u32[]{:S(2)}) copy-start(f32[64,32]{0,1:T(8,128)S(1)} %get-tuple-element.69) | copy-start | bytes 24580
  547.5 38.2 all-to-all-start
  569.2 71.2 %copy-start = (f32[32,64,256]{2,0,1:T(8,128)}, f32[32,64,256]{2,0,1:T(8,128)S(1)}, u32[]{:S(2)}) copy-start(f32[32,64,256]{2,0,1:T(8,128)S(1)} %subtract_bitcast_fusion.3) | copy-start | bytes 6291460
  618.8 21.5 copy-start.3
  618.8 6.7 copy-start.8
  625.5 14.8 copy-start.5
  666.8 13.9 copy-start.60
  666.8 291.1 %copy-start.24 = (bf16[2,128,2048]{2,1,0:T(8,128)(2,1)S(1)}, bf16[2,128,2048]{2,1,0:T(8,128)(2,1)}, u32[]{:S(2)}) copy-start(bf16[2,128,2048]{2,1,0:T(8,128)(2,1)} %param.25) | copy-start | bytes 3145732
  669.1 302.3 %all-to-all-start.1 = ((bf16[2,1024,256]{2,0,1:T(2,128)(2,1)}), bf16[2,1024,256]{2,0,1:T(2,128)(2,1)S(1)}, u32[]{:S(2)}, u32[]{:S(2)}) async-start(bf16[2,1024,256]{2,0,1:T(2,128)(2,1)} %copy.186), calls=%async_computation.1 | async-start | bytes 2097152 | tf_op jit(solution)/shard_map/all_to_all | solution.py:162
  680.6 1663.7 %reduce-scatter.8.cloned.1.call-start = ((), (), s32[]{:S(2)}) async-start(), calls=%async_computation.15 | async-start | bytes 9437184 | tf_op jit(solution)/shard_map/reduce_scatter | solution.py:241
  976.2 116.0 %copy-start.52 = (f32[2048]{0:T(1024)S(1)}, f32[2048]{0:T(1024)}, u32[]{:S(2)}) copy-start(f32[2048]{0:T(1024)} %param.21) | copy-start | bytes 24580
  1092.1 909.9 %copy-start.21 = (f32[2,128,2048]{2,1,0:T(8,128)}, f32[2,128,2048]{2,1,0:T(8,128)S(1)}, u32[]{:S(2)}) copy-start(f32[2,128,2048]{2,1,0:T(8,128)S(1)} %get-tuple-element.62) | copy-start | bytes 6291460
  2015.8 3.4 copy-start.23
  2019.2 46.6 %copy-start.11 = (f32[2,128,2048]{2,1,0:T(8,128)}, f32[2,128,2048]{2,1,0:T(8,128)S(1)}, u32[]{:S(2)}) copy-start(f32[2,128,2048]{2,1,0:T(8,128)S(1)} %subtract_add_fusion) | copy-start | bytes 6291460
  2025.0 570.4 %reduce-scatter.10.cloned.1.call-start = ((), (), s32[]{:S(2)}) async-start(), calls=%async_computation.16 | async-start | bytes 25952256 | tf_op jit(solution)/shard_map/reduce_scatter | solution.py:187
  2038.1 933.8 %reduce-scatter.12.cloned.1.call-start = ((), (), s32[]{:S(2)}) async-start(), calls=%async_computation.17 | async-start | bytes 25952256 | tf_op jit(solution)/shard_map/reduce_scatter | solution.py:190
  2051.4 1297.5 %reduce-scatter.14.cloned.1.call-start = ((), (), s32[]{:S(2)}) async-start(), calls=%async_computation.18 | async-start | bytes 25952256 | tf_op jit(solution)/shard_map/reduce_scatter | solution.py:193
  2065.8 1690.4 %reduce-scatter.6.cloned.1.call-start = ((), (), s32[]{:S(2)}) async-start(), calls=%async_computation.14 | async-start | bytes 28311552 | tf_op jit(solution)/shard_map/reduce_scatter | solution.py:238
  2133.3 14.2 copy-start.9
  2147.5 6.7 copy-start.4
  2147.5 6.7 copy-start.6
  2154.2 15.7 copy-start.1
  2169.9 6.5 copy-start.7
  2180.7 6.0 copy-start.31
  2180.7 6.0 copy-start.33
  2213.4 59.3 %slice-start = ((s8[6291456]{0:T(1024)(128)(4,1)}), s8[4194304]{0:T(1024)(128)(4,1)S(1)}, s32[]{:S(2)}) async-start(s8[6291456]{0:T(1024)(128)(4,1)} %bitcast.429), calls=%async_computation.22 | async-start | bytes 8388608
  2274.7 8.5 copy-start.14
  2274.7 8.5 copy-start.15
  2276.0 7.2 collective-permute-start.1
  2283.2 3.4 copy-start.42
  2283.2 3.4 copy-start.44
  2283.2 3.4 copy-start.46
  2286.7 18.0 copy-start.20
  2286.7 18.0 copy-start.48
  2286.7 18.0 copy-start.51
  2318.5 1513.2 %all-reduce.12.cloned.1.call-start = ((), (), s32[]{:S(2)}) async-start(), calls=%async_computation.19 | async-start | bytes 720896 | tf_op jit(solution)/shard_map/psum | solution.py:261
  2318.6 3.8 copy-start.17
  2344.3 1716.3 %all-reduce.16.cloned.1.call-start = ((), (), s32[]{:S(2)}) async-start(), calls=%async_computation.21 | async-start | bytes 25690112 | tf_op jit(solution)/shard_map/psum | solution.py:263
  3756.2 339.8 %all-reduce.14.cloned.1.call-start = ((), (), s32[]{:S(2)}) async-start(), calls=%async_computation.20 | async-start | bytes 720896 | tf_op jit(solution)/shard_map/psum | solution.py:261
  3770.1 61.6 %copy-start.12 = (f32[2,128,2048]{2,1,0:T(8,128)S(1)}, f32[2,128,2048]{2,1,0:T(8,128)}, u32[]{:S(2)}) copy-start(f32[2,128,2048]{2,1,0:T(8,128)} %copy-done.11) | copy-start | bytes 6291460
  3784.1 51.0 %copy-start.57 = (f32[2048]{0:T(1024)S(1)}, f32[2048]{0:T(1024)}, u32[]{:S(2)}) copy-start(f32[2048]{0:T(1024)} %get-tuple-element.17) | copy-start | bytes 24580
  4060.6 5.5 copy-start.29
  4066.0 3.2 copy-start.28
  4069.3 3.2 copy-start.27
  4072.5 3.3 copy-start.34
  (16 other events, 28.1 us)
Sparse Core Ops, SparseCore 0:
  9.5 483.1 all-gather.5
  494.2 463.6 all-gather.13
  960.0 125.8 all-gather.7
  1087.3 439.2 all-gather.11
  1528.0 441.0 all-gather.9
  2025.1 169.6 reduce-scatter.7
  2199.2 396.1 reduce-scatter.9
  2599.7 372.1 reduce-scatter.11
  2976.3 372.6 reduce-scatter.13
  3353.2 402.9 reduce-scatter.5
  3760.8 70.8 all-reduce.11
  3834.6 225.8 all-reduce.15
  4063.1 32.8 all-reduce.13
